TPU v7x, 256 devices: a whole 4x4x8 slice. The times are simulated.
256 devices in a mesh: section: 16 (over y_hi, z), fsdp: 16 (over y_lo, x, core).
Axes of the slice: x: 4, y: 4 (y_hi: 2, y_lo: 2; y = y_hi * 2 + y_lo), z: 8, core: 2. Of those that a mesh axis runs over, the one named last changes fastest.
Arguments:
- patch_rows: bfloat16 [16, 2048, 1280], P('section', 'fsdp'), may hold values from -6 to 6
- query: bfloat16 [16, 2048, 640], P('section', 'fsdp'), may hold values from -32 to 32
- key_rows: bfloat16 [16, 2048, 640], P('section', 'fsdp'), may hold values from -32 to 32
- value_rows: bfloat16 [16, 2048, 640], P('section', 'fsdp'), may hold values from -6 to 6
- image_lengths: int32 [16, 4], P('section'), may hold values from 1 to 256, 512 in all within a row
- token_slots: int32 [16, 512], P('section', 'fsdp'), may hold values from 0 to 2047, as said below
- out_proj: bfloat16 [640, 1280], P('fsdp'), may hold values from -0.25 to 0.25
- merge_gain: float32 [1280], replicated, may hold values from 0.1 to 1.9
- merger_weight: bfloat16 [5120, 4096], P('section', 'fsdp'), may hold values from -0.078125 to 0.078125
- text_rows: bfloat16 [16, 2048, 4096], P('section', 'fsdp'), may hold values from -6 to 6
- norm_gain: float32 [4096], replicated, may hold values from 0.1 to 1.9
- out_grad: bfloat16 [16, 2048, 4096], P('section', 'fsdp'), may hold values from -6 to 6
Outputs:
- llm_input: bfloat16 [16, 2048, 4096], P('section', 'fsdp')
- grad_patches: bfloat16 [16, 2048, 1280], P('section', 'fsdp')
- grad_query: bfloat16 [16, 2048, 640], P('section', 'fsdp')
- grad_key: bfloat16 [16, 2048, 640], P('section', 'fsdp')
- grad_value: bfloat16 [16, 2048, 640], P('section', 'fsdp')
- grad_norm_gain: float32 [4096], replicated
- grad_merge_gain: float32 [1280], replicated
- grad_merger: float32 [5120, 4096], P('section', 'fsdp')
- grad_out_proj: float32 [640, 1280], P('fsdp')
Inputs may be any that keep to these rules, and one draw needn't show every extreme that they name: `token_slots`: within a micro-batch the values are distinct, and every block of 128 consecutive token rows receives exactly 32 of them.
All inputs are finite; a program needn't handle non-finite values.
Results may differ from a plain program's by a relative error of at most 0.03.
Values may be sent and summed in bfloat16 or wider, within the bound.
No kernel may reach another device: no remote copies, remote signals or barrier semaphores. Data moves between devices by JAX's collectives and lax.ppermute only.
A program may use at most 128 MiB of HBM per device.

v0:
```python
import jax
import jax.numpy as jnp
from jax import lax
from jax.sharding import Mesh
from jax.sharding import PartitionSpec as P

HEAD_DIM = 80
FSDP = ("fsdp_0", "fsdp_1", "fsdp_2")
SECTION = ("section_0", "section_1")
SECTION_FSDP = ("section_0", "section_1", "fsdp_0", "fsdp_1", "fsdp_2")
EPS = 1e-06


def sent_together(arrays, axis, dim, along):
    widths = [a.shape[along] for a in arrays]
    both = jnp.concatenate(arrays, axis=along)
    result = lax.all_gather(both, axis, axis=dim, tiled=True)
    return tuple(jnp.split(result, [sum(widths[:k]) for k in range(1, len(widths))], axis=along))


def in_order(pieces, dim):
    dims = list(pieces.shape[1:])
    dims[dim] *= pieces.shape[0]
    return jnp.moveaxis(pieces, 0, dim).reshape(dims)


def sent_to_all(x, axis):
    copies = jnp.broadcast_to(x, (lax.axis_size(axis), *x.shape))
    return lax.all_to_all(copies, axis, split_axis=0, concat_axis=0, tiled=True)


def gathered_copies(x, axis, dim):
    return in_order(sent_to_all(x, axis), dim)


def in_blocks(x, dim, count):
    dims = x.shape
    pieces = x.reshape(*dims[:dim], count, dims[dim] // count, *dims[dim + 1 :])
    return jnp.moveaxis(pieces, dim, 0)


def sum_at_owner(x, axis, dim):
    pieces = in_blocks(x, dim, lax.axis_size(axis))
    arrived = lax.all_to_all(pieces, axis, split_axis=0, concat_axis=0, tiled=True)
    return arrived.astype(jnp.float32).sum(axis=0)


def reduced_to_own(pieces, axes, sequence):
    inside = pieces.shape[1:]
    pieces = pieces.reshape(*(lax.axis_size(a) for a in axes), *inside)
    pieces = jnp.moveaxis(pieces, sequence, range(len(axes))).reshape(-1, *inside)
    for k in sequence:
        pieces = lax.psum_scatter(pieces, axes[k], scatter_dimension=0, tiled=True)
    return pieces[0]


def summed_rows(x, axes, sequence, dim):
    count = lax.axis_size(axes)
    return reduced_to_own(in_blocks(x, dim, count), axes, sequence)


def over_copies(x, axis):
    return sent_to_all(x, axis).astype(jnp.float32).sum(axis=0)


def over_axes(x, axes):
    for axis in axes:
        x = lax.psum(x, axis)
    return x


def sent_together_2(arrays, axis, dim, along):
    ends, at = ([], 0)
    for a in arrays[:-1]:
        at += a.shape[along]
        ends.append(at)
    both = jnp.concatenate(arrays, axis=along)
    return tuple(
        jnp.split(lax.psum_scatter(both, axis, scatter_dimension=dim, tiled=True), ends, axis=along)
    )


def image_ids(ends, index):
    merged_index = index // 4
    return jnp.sum((merged_index[:, None] >= ends[None, :]).astype(jnp.int32), axis=1)


def split_heads(rows):
    return rows.reshape(rows.shape[0], -1, HEAD_DIM)


def whole_probs(query_heads, key_heads, mask):
    scale = HEAD_DIM ** (-0.5)
    scores = (
        jnp.einsum("qhd,khd->hqk", query_heads, key_heads, preferred_element_type=jnp.float32)
        * scale
    )
    scores = jnp.where(mask[None], scores, -jnp.inf)
    top = jnp.max(scores, axis=-1, keepdims=True)
    weights = jnp.where(mask[None], jnp.exp(scores - top), 0.0)
    return (weights / jnp.sum(weights, axis=-1, keepdims=True), scale)


def on_device(
    patch_rows,
    query,
    key_rows,
    value_rows,
    image_lengths,
    token_slots,
    out_proj,
    merge_gain,
    merger_weight,
    text_rows,
    norm_gain,
    out_grad,
):
    patches = patch_rows[0]
    rows, width = patches.shape
    att_width = query.shape[2]
    place = lax.axis_index(FSDP)
    groups = lax.axis_size(FSDP)
    ends = jnp.cumsum(image_lengths[0])
    own_index = place * rows + jnp.arange(rows, dtype=jnp.int32)
    all_index = jnp.arange(rows * groups, dtype=jnp.int32)
    mask = image_ids(ends, own_index)[:, None] == image_ids(ends, all_index)[None, :]
    keys_all, values_all = sent_together((key_rows[0], value_rows[0]), FSDP, 0, 1)
    query_heads = split_heads(query[0])
    key_heads = split_heads(keys_all)
    value_heads = split_heads(values_all)
    probs, scale = whole_probs(query_heads, key_heads, mask)
    probs_low = probs.astype(jnp.bfloat16)
    attended = jnp.einsum(
        "hqk,khd->qhd", probs_low, value_heads, preferred_element_type=jnp.float32
    )
    attended = attended.reshape(rows, att_width).astype(jnp.bfloat16)
    proj_full = gathered_copies(out_proj, FSDP, 0)
    mixed = patches.astype(jnp.float32) + jnp.dot(
        attended, proj_full, preferred_element_type=jnp.float32
    )
    centre = mixed - jnp.mean(mixed, axis=-1, keepdims=True)
    inv_std = lax.rsqrt(jnp.mean(centre * centre, axis=-1, keepdims=True) + EPS)
    unit = centre * inv_std
    normed = (unit * merge_gain).astype(jnp.bfloat16)
    merged_local = normed.reshape(rows // 4, 4 * width)
    merged_all, slots_all = (
        lax.all_gather(merged_local, FSDP, axis=0, tiled=True),
        lax.all_gather(token_slots[0], FSDP, axis=0, tiled=True),
    )
    merger_cols = lax.all_gather(merger_weight, SECTION, axis=0, tiled=True)
    projected = jnp.dot(merged_all, merger_cols, preferred_element_type=jnp.float32).astype(
        jnp.bfloat16
    )
    order = jnp.argsort(slots_all)
    inverse = jnp.argsort(order)
    sorted_slots = slots_all[order]
    mine = lax.all_to_all(projected[order], FSDP, split_axis=0, concat_axis=1, tiled=True)
    count = mine.shape[0]
    text = text_rows[0]
    tokens = text.shape[0]
    local_rows = lax.dynamic_slice_in_dim(sorted_slots, place * count, count) - place * tokens
    stream = text.at[local_rows].set(mine).astype(jnp.float32)
    inv_rms = lax.rsqrt(jnp.mean(stream * stream, axis=-1, keepdims=True) + EPS)
    scaled = stream * inv_rms
    llm_input = (scaled * norm_gain).astype(jnp.bfloat16)
    upstream_raw = out_grad[0].astype(jnp.float32)
    norm_gain_part = jnp.sum(upstream_raw * scaled, axis=0)
    upstream = upstream_raw * norm_gain
    stream_grad = inv_rms * (
        upstream - scaled * jnp.mean(upstream * scaled, axis=-1, keepdims=True)
    )
    image_grad = stream_grad[local_rows].astype(jnp.bfloat16)
    returned = lax.all_to_all(image_grad, FSDP, split_axis=1, concat_axis=0, tiled=True)[inverse]
    block = lax.slice_in_dim(returned, 0, merged_local.shape[0] * lax.axis_size(FSDP), axis=0)
    merged_grad = sum_at_owner(
        jnp.dot(block, merger_cols.T, preferred_element_type=jnp.float32).astype(jnp.bfloat16),
        FSDP,
        0,
    )
    block = merged_all
    merger_grad = summed_rows(
        jnp.dot(block.T, returned, preferred_element_type=jnp.float32).astype(jnp.bfloat16),
        SECTION,
        (1, 0),
        0,
    ).astype(jnp.float32)
    normed_grad = merged_grad.reshape(rows, width)
    merge_gain_part = jnp.sum(normed_grad * unit, axis=0)
    unit_grad = normed_grad * merge_gain
    mixed_grad = inv_std * (
        unit_grad
        - jnp.mean(unit_grad, axis=-1, keepdims=True)
        - unit * jnp.mean(unit_grad * unit, axis=-1, keepdims=True)
    )
    mixed_low = mixed_grad.astype(jnp.bfloat16)
    block = attended
    proj_part = sum_at_owner(
        jnp.dot(block.T, mixed_low, preferred_element_type=jnp.float32).astype(jnp.bfloat16),
        FSDP,
        0,
    )
    proj_grad = over_copies(proj_part.astype(jnp.bfloat16), SECTION).astype(jnp.float32)
    norm_total, merge_total = (
        over_axes(norm_gain_part, SECTION_FSDP),
        over_axes(merge_gain_part, SECTION_FSDP),
    )
    attended_grad = jnp.dot(mixed_low, proj_full.T, preferred_element_type=jnp.float32).astype(
        jnp.bfloat16
    )
    grad_heads = split_heads(attended_grad)
    value_grad = jnp.einsum(
        "hqk,qhd->khd", probs_low, grad_heads, preferred_element_type=jnp.float32
    )
    prob_grad = jnp.einsum(
        "qhd,khd->hqk", grad_heads, value_heads, preferred_element_type=jnp.float32
    )
    score_grad = probs * (prob_grad - jnp.sum(prob_grad * probs, axis=-1, keepdims=True))
    score_low = (score_grad * scale).astype(jnp.bfloat16)
    query_grad = jnp.einsum(
        "hqk,khd->qhd", score_low, key_heads, preferred_element_type=jnp.float32
    ).reshape(rows, att_width)
    key_grad = jnp.einsum(
        "hqk,qhd->khd", score_low, query_heads, preferred_element_type=jnp.float32
    )
    total_rows = key_grad.shape[0]
    key_own, value_own = tuple(
        (
            part.astype(jnp.float32)
            for part in sent_together_2(
                (
                    key_grad.reshape(total_rows, att_width).astype(jnp.bfloat16),
                    value_grad.reshape(total_rows, att_width).astype(jnp.bfloat16),
                ),
                FSDP,
                0,
                1,
            )
        )
    )
    return (
        llm_input[None],
        mixed_low[None],
        query_grad.astype(jnp.bfloat16)[None],
        key_own.astype(jnp.bfloat16)[None],
        value_own.astype(jnp.bfloat16)[None],
        norm_total,
        merge_total,
        merger_grad,
        proj_grad,
    )


def solution(mesh):
    torus = Mesh(
        mesh.devices.reshape(2, 8, 2, 4, 2),
        ("section_0", "section_1", "fsdp_0", "fsdp_1", "fsdp_2"),
    )
    placed = (
        P(SECTION, FSDP, None),
        P(SECTION, FSDP, None),
        P(SECTION, FSDP, None),
        P(SECTION, FSDP, None),
        P(SECTION, None),
        P(SECTION, FSDP),
        P(FSDP, None),
        P(),
        P(SECTION, FSDP),
        P(SECTION, FSDP, None),
        P(),
        P(SECTION, FSDP, None),
    )
    return jax.shard_map(
        on_device,
        mesh=torus,
        in_specs=placed,
        out_specs=(
            P(SECTION, FSDP, None),
            P(SECTION, FSDP, None),
            P(SECTION, FSDP, None),
            P(SECTION, FSDP, None),
            P(SECTION, FSDP, None),
            P(),
            P(),
            P(SECTION, FSDP),
            P(FSDP, None),
        ),
        check_vma=False,
    )
```

profile of v0, /device:TPU:1, one launch (start us, length us, event | category | flops | bytes accessed | tf_op | source)
XLA Modules:
  0.0 517.0 jit_solution(1756903741598296426)
XLA Ops:
  7.2 1.8 pad_maximum_fusion.1
  9.1 0.7 all-gather.9.cloned.1.call-update
  9.8 2.2 broadcast_in_dim.74
  12.0 6.8 %all-to-all-start = ((bf16[16,40,1280]{2,1,0:T(8,128)(2,1)}), bf16[16,40,1280]{2,1,0:T(8,128)(2,1)S(1)}, u32[]{:S(2)}, u32[]{:S(2)}) async-start(bf16[16,40,1280]{2,1,0:T(8,128)(2,1)} %broadcast_in_dim.74), calls=%async_computation | async-start | bytes 3276800 | tf_op jit(solution)/shard_map/all_to_all | solution.py:29
  19.4 0.3 broadcast_compare_fusion
  19.8 47.4 %all-gather.5.cloned.1.call-done = bf16[2048,1280]{1,0:T(8,128)(2,1)} async-done(((bf16[128,1280]{1,0:T(8,128)(2,1)}), bf16[2048,1280]{1,0:T(8,128)(2,1)}) %all-gather.5.cloned.1.call-update) | async-done | bytes 5242896 | tf_op jit(solution)/shard_map/all_gather | solution.py:17
  67.2 5.3 %fusion.48 = (bf16[2048,640]{1,0:T(8,128)(2,1)}, bf16[2048,640]{1,0:T(8,128)(2,1)}) fusion(bf16[2048,1280]{1,0:T(8,128)(2,1)} %all-gather.5.cloned.1.call-done), kind=kLoop, calls=%fused_computation.95 | loop fusion | bytes 10485760 | tf_op jit(solution)/shard_map/split | solution.py:18
  72.5 4.6 copy.72
  77.0 4.5 copy.71
  81.5 8.7 %fusion.49 = (f32[8,128]{1,0:T(8,128)S(1)}, f32[8,128,2048]{1,2,0:T(8,128)}) fusion(pred[128,2048]{0,1:T(8,128)(4,1)S(1)} %broadcast_compare_fusion, bf16[2048,8,80]{0,2,1:T(8,128)(2,1)} %bitcast.104, bf16[128,8,80]{0,2,1:T(8,128)(2,1)S(1)} %bitcast.118), kind=kOutput, calls=%fused_computation.96 | convolution fusion | flops 346032128 | bytes 11440128 | tf_op jit(solution)/shard_map/sub | solution.py:100
  90.2 5.2 %fusion.30 = bf16[8,80,128]{2,1,0:T(8,128)(2,1)S(1)} fusion(bf16[2048,8,80]{0,2,1:T(8,128)(2,1)} %bitcast.100, f32[8,128,2048]{1,2,0:T(8,128)} %get-tuple-element.70, f32[8,128]{1,0:T(8,128)S(1)} %get-tuple-element.69), kind=kOutput, calls=%fused_computation.45 | convolution fusion | flops 339820544 | bytes 11177984 | tf_op jit(solution)/shard_map/hqk,khd->qhd/dot_general | solution.py:133
  95.4 1.2 copy-done.1
  96.7 2.0 fusion.50
  99.1 0.9 reshape.203
  100.0 0.6 dynamic-slice
  101.4 8.4 %all-reduce = s32[512]{0:T(512)S(1)} all-reduce(s32[512]{0:T(512)S(1)} %bitcast_dynamic-update-slice_fusion), channel_id=2, replica_groups=mesh['section_0'=2,'section_1'=8,'fsdp_0'=2,'fsdp_1'=4,'fsdp_2'=2] {'fsd..., use_global_device_ids=true, to_apply=%add | all-reduce | flops 512 | bytes 4096 | tf_op jit(solution)/shard_map/all_gather | solution.py:148
  109.8 3.8 sort.31
  113.6 42.9 %all-gather.9.cloned.1.call-done = bf16[5120,256]{1,0:T(8,128)(2,1)} async-done(((bf16[320,256]{1,0:T(8,128)(2,1)}), bf16[5120,256]{1,0:T(8,128)(2,1)}) %all-gather.9.cloned.1.call-update) | async-done | bytes 2621456 | tf_op jit(solution)/shard_map/all_gather | solution.py:150
  156.5 44.9 %all-gather.7.cloned.1.call-done = bf16[512,5120]{1,0:T(8,128)(2,1)} async-done(((bf16[32,5120]{1,0:T(8,128)(2,1)}), bf16[512,5120]{1,0:T(8,128)(2,1)}) %all-gather.7.cloned.1.call-update) | async-done | bytes 5242896 | tf_op jit(solution)/shard_map/all_gather | solution.py:147
  201.4 4.8 convolution_convert_fusion.4
  206.2 2.6 gather_fusion.1
  208.8 3.8 all-to-all-start.1
  212.6 3.5 gather_fusion
  216.1 3.8 sort.32
  220.0 1.7 scatter_fusion
  221.7 0.3 fusion.25
  222.0 1.8 fusion.26
  223.9 0.6 fusion.22
  224.5 0.7 gather_fusion.2
  225.2 0.7 copy.95
  225.9 5.7 %all-to-all-start.2 = ((bf16[32,16,256]{2,0,1:T(8,128)(2,1)}), bf16[32,16,256]{2,0,1:T(8,128)(2,1)S(1)}, u32[]{:S(2)}, u32[]{:S(2)}) async-start(bf16[32,16,256]{2,0,1:T(8,128)(2,1)} %bitcast.92), calls=%async_computation.2 | async-start | bytes 524288 | tf_op jit(solution)/shard_map/all_to_all | solution.py:173
  231.6 7.2 %all-to-all-done.2 = bf16[32,16,256]{2,0,1:T(8,128)(2,1)S(1)} async-done(((bf16[32,16,256]{2,0,1:T(8,128)(2,1)}), bf16[32,16,256]{2,0,1:T(8,128)(2,1)S(1)}, u32[]{:S(2)}, u32[]{:S(2)}) %all-to-all-start.2) | async-done | bytes 262176 | tf_op jit(solution)/shard_map/all_to_all | solution.py:173
  238.8 1.9 gather_fusion.3
  240.8 5.7 %convolution_convert_fusion = bf16[512,5120]{1,0:T(8,128)(2,1)} fusion(bf16[512,256]{1,0:T(8,128)(2,1)S(1)} %gather_fusion.3, bf16[5120,256]{1,0:T(8,128)(2,1)} %all-gather.9.cloned.1.call-done), kind=kOutput, calls=%fused_computation.13 | convolution fusion | flops 1344798720 | bytes 8126464 | tf_op jit(solution)/shard_map/dot_general | solution.py:176
  246.5 5.1 all-to-all-start.3
  251.6 4.1 convolution_convert_fusion.1
  255.7 1.7 copy.85
  257.3 0.3 reduce-scatter.8.cloned.1.call-start
  257.6 63.6 %all-to-all-done.3 = bf16[16,32,5120]{2,1,0:T(8,128)(2,1)} async-done(((bf16[16,32,5120]{2,1,0:T(8,128)(2,1)}), bf16[16,32,5120]{2,1,0:T(8,128)(2,1)}, u32[]{:S(2)}, u32[]{:S(2)}) %all-to-all-start.3) | async-done | bytes 5242912 | tf_op jit(solution)/shard_map/all_to_all | solution.py:44
  321.2 3.5 convert_reduce_fusion
  324.9 0.3 multiply_reduce_fusion.1
  325.2 0.3 multiply_convert_fusion.1
  325.5 2.2 convolution_convert_fusion.5
  327.9 6.5 %convolution_convert_fusion.3 = bf16[8,80,2048]{2,1,0:T(8,128)(2,1)} fusion(bf16[128,8,80]{0,2,1:T(8,128)(2,1)S(1)} %bitcast.114, f32[8,128,2048]{1,2,0:T(8,128)} %get-tuple-element.70, f32[8,128]{1,0:T(8,128)S(1)} %get-tuple-element.69), kind=kOutput, calls=%fused_computation.26 | convolution fusion | flops 341049344 | bytes 11177984 | tf_op jit(solution)/shard_map/hqk,qhd->khd/dot_general | solution.py:211
  334.4 3.1 copy.84
  337.5 6.4 %fusion.51 = f32[8,128,2048]{1,2,0:T(8,128)} fusion(bf16[128,8,80]{0,2,1:T(8,128)(2,1)S(1)} %bitcast.115, bf16[2048,8,80]{0,2,1:T(8,128)(2,1)} %bitcast.101), kind=kOutput, calls=%fused_computation.98 | convolution fusion | flops 335544320 | bytes 11173888 | tf_op jit(solution)/shard_map/qhd,khd->hqk/dot_general | solution.py:214
  344.0 14.6 %fusion.15 = bf16[8,2048,80]{1,2,0:T(8,128)(2,1)} fusion(bf16[128,8,80]{0,2,1:T(8,128)(2,1)S(1)} %bitcast.119, f32[8,128,2048]{1,2,0:T(8,128)} %fusion.51, f32[8,128,2048]{1,2,0:T(8,128)} %get-tuple-element.70, f32[8,128]{1,0:T(8,128)S(1)} %get-tuple-element.69), kind=kOutput, calls=%fused_computation.24 | convolution fusion | flops 351538176 | bytes 19566592 | tf_op jit(solution)/shard_map/hqk,qhd->khd/dot_general | solution.py:222
  358.6 4.4 copy.83
  363.0 4.4 pad_maximum_fusion
  367.5 0.6 convolution_convert_fusion.2
  368.1 28.9 %all_to_all.55 = bf16[16,40,1280]{2,1,0:T(8,128)(2,1)S(1)} all-to-all(bf16[16,40,1280]{2,1,0:T(8,128)(2,1)S(1)} %bitcast.102), channel_id=1, replica_groups=mesh['section_0'=2,'section_1'=8,'fsdp_0'=2,'fsdp_1'=4,'fsdp_2'=2] {'fsd..., dimensions={0} | all-to-all | bytes 3276800 | tf_op jit(solution)/shard_map/all_to_all | solution.py:44
  396.9 0.3 reduce_sum.151
  397.2 1.3 broadcast_in_dim.80
  398.5 9.2 %all-to-all-start.5 = ((bf16[16,40,1280]{2,1,0:T(8,128)(2,1)}), bf16[16,40,1280]{2,1,0:T(8,128)(2,1)S(1)}, u32[]{:S(2)}, u32[]{:S(2)}) async-start(bf16[16,40,1280]{2,1,0:T(8,128)(2,1)} %broadcast_in_dim.80), calls=%async_computation.8 | async-start | bytes 3276800 | tf_op jit(solution)/shard_map/all_to_all | solution.py:29
  407.7 14.6 %fusion.33 = bf16[8,80,128]{2,1,0:T(8,128)(2,1)S(1)} fusion(bf16[2048,8,80]{0,2,1:T(8,128)(2,1)} %bitcast.105, f32[8,128,2048]{1,2,0:T(8,128)} %fusion.51, f32[8,128,2048]{1,2,0:T(8,128)} %get-tuple-element.70, f32[8,128]{1,0:T(8,128)S(1)} %get-tuple-element.69), kind=kOutput, calls=%fused_computation.46 | convolution fusion | flops 350309376 | bytes 19566592 | tf_op jit(solution)/shard_map/hqk,khd->qhd/dot_general | solution.py:219
  422.3 0.8 copy.86
  423.2 21.3 %all-reduce.5 = (f32[4096]{0:T(1024)S(1)}, f32[1280]{0:T(1024)S(1)}) all-reduce(f32[4096]{0:T(1024)S(1)} %get-tuple-element.49, f32[1280]{0:T(1024)S(1)} %get-tuple-element.51), channel_id=1, replica_groups=mesh['section_0'=2,'section_1'=8,'fsdp_0'=2,'fsdp_1'=4,'fsdp_2'=2] {'sec..., use_global_device_ids=true, to_apply=%region_18.19 | all-reduce | flops 5376 | bytes 43008 | tf_op jit(solution)/shard_map/psum | solution.py:68
  444.4 23.7 %all-reduce.1 = (f32[4096]{0:T(1024)S(1)}, f32[1280]{0:T(1024)S(1)}) all-reduce(f32[4096]{0:T(1024)S(1)} %get-tuple-element.62, f32[1280]{0:T(1024)S(1)} %get-tuple-element.63), channel_id=1, replica_groups=mesh['section_0'=2,'section_1'=8,'fsdp_0'=2,'fsdp_1'=4,'fsdp_2'=2] {'sec..., use_global_device_ids=true, to_apply=%region_19.20 | all-reduce | flops 5376 | bytes 43008 | tf_op jit(solution)/shard_map/psum | solution.py:68
  468.1 6.1 %all-reduce.4 = (f32[4096]{0:T(1024)S(1)}, f32[1280]{0:T(1024)S(1)}) all-reduce(f32[4096]{0:T(1024)S(1)} %get-tuple-element.54, f32[1280]{0:T(1024)S(1)} %get-tuple-element.55), channel_id=1, replica_groups=mesh['section_0'=2,'section_1'=8,'fsdp_0'=2,'fsdp_1'=4,'fsdp_2'=2] {'fsd..., use_global_device_ids=true, to_apply=%region_20.21 | all-reduce | flops 5376 | bytes 43008 | tf_op jit(solution)/shard_map/psum | solution.py:68
  474.2 12.4 %all-reduce.2 = (f32[4096]{0:T(1024)S(1)}, f32[1280]{0:T(1024)S(1)}) all-reduce(f32[4096]{0:T(1024)S(1)} %get-tuple-element.60, f32[1280]{0:T(1024)S(1)} %get-tuple-element.61), channel_id=1, replica_groups=mesh['section_0'=2,'section_1'=8,'fsdp_0'=2,'fsdp_1'=4,'fsdp_2'=2] {'fsd..., use_global_device_ids=true, to_apply=%region_21.22 | all-reduce | flops 5376 | bytes 43008 | tf_op jit(solution)/shard_map/psum | solution.py:68
  486.6 19.2 %all-reduce.3 = (f32[4096]{0:T(1024)}, f32[1280]{0:T(1024)}) all-reduce(f32[4096]{0:T(1024)S(1)} %get-tuple-element.56, f32[1280]{0:T(1024)S(1)} %get-tuple-element.57), channel_id=1, replica_groups=mesh['section_0'=2,'section_1'=8,'fsdp_0'=2,'fsdp_1'=4,'fsdp_2'=2] {'fsd..., use_global_device_ids=true, to_apply=%region_22.23 | all-reduce | flops 5376 | bytes 43008 | tf_op jit(solution)/shard_map/psum | solution.py:68
  505.8 1.7 bitcast_convert_fusion
  507.5 0.9 convert_reduce_fusion.1
  508.4 1.7 slice_bitcast_fusion
  (69 shorter events, 1.9 us)
Async XLA Ops:
  7.2 11.7 %copy-start.6 = (bf16[1,128,640]{2,1,0:T(8,128)(2,1)S(1)}, bf16[1,128,640]{2,1,0:T(8,128)(2,1)}, u32[]{:S(2)}) copy-start(bf16[1,128,640]{2,1,0:T(8,128)(2,1)} %param.13) | copy-start | bytes 491524
  7.2 11.9 %copy-start.11 = (s32[1,4]{1,0:T(1,128)S(1)}, s32[1,4]{1,0:T(1,128)}, u32[]{:S(2)}) copy-start(s32[1,4]{1,0:T(1,128)} %param.16) | copy-start | bytes 52
  7.2 60.0 %all-gather.5.cloned.1.call-start = ((), (), s32[]{:S(2)}) async-start(), calls=%async_computation.9 | async-start | bytes 5570560 | tf_op jit(solution)/shard_map/all_gather | solution.py:17
  9.0 147.4 %all-gather.9.cloned.1.call-start = ((), (), s32[]{:S(2)}) async-start(), calls=%async_computation.11 | async-start | bytes 2785280 | tf_op jit(solution)/shard_map/all_gather | solution.py:150
  12.0 83.5 %all-to-all-start = ((bf16[16,40,1280]{2,1,0:T(8,128)(2,1)}), bf16[16,40,1280]{2,1,0:T(8,128)(2,1)S(1)}, u32[]{:S(2)}, u32[]{:S(2)}) async-start(bf16[16,40,1280]{2,1,0:T(8,128)(2,1)} %broadcast_in_dim.74), calls=%async_computation | async-start | bytes 3276800 | tf_op jit(solution)/shard_map/all_to_all | solution.py:29
  18.8 182.6 %all-gather.7.cloned.1.call-start = ((), (), s32[]{:S(2)}) async-start(), calls=%async_computation.10 | async-start | bytes 5570560 | tf_op jit(solution)/shard_map/all_gather | solution.py:147
  19.0 62.5 %copy-start.7 = (bf16[1,128,640]{1,2,0:T(8,128)(2,1)}, bf16[1,128,640]{1,2,0:T(8,128)(2,1)S(1)}, u32[]{:S(2)}) copy-start(bf16[1,128,640]{1,2,0:T(8,128)(2,1)S(1)} %copy.73) | copy-start | bytes 491524
  90.2 6.5 %copy-start.5 = (bf16[1,128,1280]{2,1,0:T(8,128)(2,1)S(1)}, bf16[1,128,1280]{2,1,0:T(8,128)(2,1)}, u32[]{:S(2)}) copy-start(bf16[1,128,1280]{2,1,0:T(8,128)(2,1)} %param.12) | copy-start | bytes 983044
  90.2 8.7 %copy-start.9 = (f32[1280]{0:T(1024)S(1)}, f32[1280]{0:T(1024)}, u32[]{:S(2)}) copy-start(f32[1280]{0:T(1024)} %param.19) | copy-start | bytes 15364
  95.4 4.6 copy-start.13
  95.4 5.9 %copy-start.12 = (s32[1,32]{1,0:T(1,128)S(1)}, s32[1,32]{1,0:T(1,128)}, u32[]{:S(2)}) copy-start(s32[1,32]{1,0:T(1,128)} %param.17) | copy-start | bytes 388
  95.4 1.2 copy-start.1
  206.2 13.8 %copy-start = (bf16[1,128,4096]{2,1,0:T(8,128)(2,1)S(1)}, bf16[1,128,4096]{2,1,0:T(8,128)(2,1)}, u32[]{:S(2)}) copy-start(bf16[1,128,4096]{2,1,0:T(8,128)(2,1)} %param.21) | copy-start | bytes 3145732
  208.8 11.1 %all-to-all-start.1 = ((bf16[16,32,256]{2,1,0:T(8,128)(2,1)}), bf16[16,32,256]{2,1,0:T(8,128)(2,1)S(1)}, u32[]{:S(2)}, u32[]{:S(2)}) async-start(bf16[16,32,256]{2,1,0:T(8,128)(2,1)} %bitcast.15), calls=%async_computation.1 | async-start | bytes 524288 | tf_op jit(solution)/shard_map/all_to_all | solution.py:157
  212.5 9.5 %copy-start.2 = (bf16[1,128,4096]{2,1,0:T(8,128)(2,1)S(1)}, bf16[1,128,4096]{2,1,0:T(8,128)(2,1)}, u32[]{:S(2)}) copy-start(bf16[1,128,4096]{2,1,0:T(8,128)(2,1)} %param.23) | copy-start | bytes 3145732
  212.5 9.5 %copy-start.10 = (f32[4096]{0:T(1024)S(1)}, f32[4096]{0:T(1024)}, u32[]{:S(2)}) copy-start(f32[4096]{0:T(1024)} %param.22) | copy-start | bytes 49156
  221.7 2.2 copy-start.3
  225.9 12.9 %all-to-all-start.2 = ((bf16[32,16,256]{2,0,1:T(8,128)(2,1)}), bf16[32,16,256]{2,0,1:T(8,128)(2,1)S(1)}, u32[]{:S(2)}, u32[]{:S(2)}) async-start(bf16[32,16,256]{2,0,1:T(8,128)(2,1)} %bitcast.92), calls=%async_computation.2 | async-start | bytes 524288 | tf_op jit(solution)/shard_map/all_to_all | solution.py:173
  246.5 74.8 %all-to-all-start.3 = ((bf16[16,32,5120]{2,1,0:T(8,128)(2,1)}), bf16[16,32,5120]{2,1,0:T(8,128)(2,1)}, u32[]{:S(2)}, u32[]{:S(2)}) async-start(bf16[16,32,5120]{2,1,0:T(8,128)(2,1)} %bitcast.95), calls=%async_computation.3 | async-start | bytes 10485760 | tf_op jit(solution)/shard_map/all_to_all | solution.py:44
  251.5 111.4 %reduce-scatter.6.cloned.1.call-start = ((), (), s32[]{:S(2)}) async-start(), calls=%async_computation.13 | async-start | bytes 2949120 | tf_op jit(solution)/shard_map/reduce_scatter | solution.py:53
  257.3 248.5 %reduce-scatter.8.cloned.1.call-start = ((), (), s32[]{:S(2)}) async-start(), calls=%async_computation.14 | async-start | bytes 491520 | tf_op jit(solution)/shard_map/reduce_scatter | solution.py:53
  325.5 42.0 %copy-start.4 = (bf16[128,1280]{1,0:T(8,128)(2,1)}, bf16[128,1280]{1,0:T(8,128)(2,1)S(1)}, u32[]{:S(2)}) copy-start(bf16[128,1280]{1,0:T(8,128)(2,1)S(1)} %multiply_convert_fusion.1) | copy-start | bytes 983044
  337.5 6.4 %copy-start.8 = (bf16[1,128,640]{1,2,0:T(8,128)(2,1)S(1)}, bf16[1,128,640]{1,2,0:T(8,128)(2,1)}, u32[]{:S(2)}) copy-start(bf16[1,128,640]{1,2,0:T(8,128)(2,1)} %copy-done.7) | copy-start | bytes 491524
  363.0 145.5 %reduce-scatter.4.cloned.1.call-start = ((), (), s32[]{:S(2)}) async-start(), calls=%async_computation.12 | async-start | bytes 5570560 | tf_op jit(solution)/shard_map/reduce_scatter | solution.py:79
  398.5 109.0 %all-to-all-start.5 = ((bf16[16,40,1280]{2,1,0:T(8,128)(2,1)}), bf16[16,40,1280]{2,1,0:T(8,128)(2,1)S(1)}, u32[]{:S(2)}, u32[]{:S(2)}) async-start(bf16[16,40,1280]{2,1,0:T(8,128)(2,1)} %broadcast_in_dim.80), calls=%async_computation.8 | async-start | bytes 3276800 | tf_op jit(solution)/shard_map/all_to_all | solution.py:29
Sparse Core Ops, SparseCore 0:
  10.4 56.7 all-gather.4
  69.8 86.6 all-gather.8
  158.9 42.4 all-gather.6
  257.5 41.4 reduce-scatter.5
  363.1 36.0 reduce-scatter.7
  401.6 71.8 reduce-scatter.3
where the time goes:
time: 518 us; the launch traced here: 517 us
  waiting for transfers between devices  207 us (40%)
  blocking collectives  120 us (23%)
  matrix products  75.3 us (15%)
  local copies, waits for them, and re-layouts  44.2 us (9%)
  starting transfers between devices  31 us (6%)
  other arithmetic  24.6 us (5%)
  between operations  15.2 us (3%)
    psum x5, blocking collectives, over_axes(): x = lax.psum(x, axis)  82.7 us
    all_to_all x1, waiting for transfers between devices, sum_at_owner(): lax.all_to_all(pieces, axis, split_axis=0, concat_axis=0, tiled=True)  63.6 us
    all_gather x1, waiting for transfers between devices, sent_together(): result = lax.all_gather(both, axis, axis=dim, tiled=True)  47.4 us
    all_gather x1, waiting for transfers between devices, on_device(): lax.all_gather(merged_local, FSDP, axis=0, tiled=True)  44.9 us
    all_gather x1, waiting for transfers between devices, on_device(): merger_cols = lax.all_gather(merger_weight, SECTION, axis=0, tiled=True)  42.9 us
    all_to_all x1, blocking collectives, sum_at_owner(): lax.all_to_all(pieces, axis, split_axis=0, concat_axis=0, tiled=True)  28.9 us
    all_to_all x2, starting transfers between devices, sent_to_all(): return lax.all_to_all(copies, axis, split_axis=0, concat_axis=0, tiled=True)  16 us
    dot_general x1, matrix products, on_device(): jnp.einsum('hqk,khd->qhd', score_low, key_heads, preferred_element_type=j...  14.6 us
  transfers between devices with their start and end apart: 11, of which 5 were waited for; matrix products, arithmetic and copies ran while one was open for 23% of the time, Pallas kernels for 0%

commit v1 on v0

--- a/solution.py
+++ b/solution.py
@@ -65,7 +65,7 @@
 
 def over_axes(x, axes):
     for axis in axes:
-        x = lax.psum(x, axis)
+        x = jnp.sum(lax.all_gather(x, axis), axis=0)
     return x
 
 

time: 518 us -> 565 us (1.091)
  blocking collectives: 120 us -> 166 us
    all_gather x0 -> x10, blocking collectives: none -> 128 us  [over_axes(): x = jnp.sum(lax.all_gather(x, axis), axis=0)]
    psum x5 -> x0, blocking collectives: 82.7 us -> none  [over_axes(): x = lax.psum(x, axis)]
  transfers between devices with their start and end apart: 11 -> 11, of which waited for: 5 -> 5; matrix products, arithmetic and copies ran while one was open for 23% -> 21% of each run, Pallas kernels for 0% -> 0%
where the time goes in v1:
time: 565 us; the launch traced here: 564 us
  waiting for transfers between devices  207 us (37%)
  blocking collectives  166 us (29%)
  matrix products  75 us (13%)
  local copies, waits for them, and re-layouts  44.3 us (8%)
  starting transfers between devices  31 us (5%)
  other arithmetic  26.1 us (5%)
  between operations  15.3 us (3%)
    all_gather x10, blocking collectives, over_axes(): x = jnp.sum(lax.all_gather(x, axis), axis=0)  128 us
    all_to_all x1, waiting for transfers between devices, sum_at_owner(): lax.all_to_all(pieces, axis, split_axis=0, concat_axis=0, tiled=True)  63.6 us
    all_gather x1, waiting for transfers between devices, sent_together(): result = lax.all_gather(both, axis, axis=dim, tiled=True)  47.4 us
    all_gather x1, waiting for transfers between devices, on_device(): lax.all_gather(merged_local, FSDP, axis=0, tiled=True)  44.9 us
    all_gather x1, waiting for transfers between devices, on_device(): merger_cols = lax.all_gather(merger_weight, SECTION, axis=0, tiled=True)  42.9 us
    all_to_all x1, blocking collectives, sum_at_owner(): lax.all_to_all(pieces, axis, split_axis=0, concat_axis=0, tiled=True)  28.9 us
    all_to_all x2, starting transfers between devices, sent_to_all(): return lax.all_to_all(copies, axis, split_axis=0, concat_axis=0, tiled=True)  16 us
    dot_general x1, matrix products, on_device(): jnp.einsum('hqk,qhd->khd', score_low, query_heads, preferred_element_type...  14.6 us
  transfers between devices with their start and end apart: 11, of which 5 were waited for; matrix products, arithmetic and copies ran while one was open for 21% of the time, Pallas kernels for 0%

profile of v1, /device:TPU:1, one launch (start us, length us, event | category | flops | bytes accessed | tf_op | source)
XLA Modules:
  0.0 564.0 jit_solution(14912115827514581697)
XLA Ops:
  7.2 1.8 pad_maximum_fusion.1
  9.1 0.7 all-gather.24.cloned.1.call-update
  9.8 2.2 broadcast_in_dim.74
  12.0 6.8 %all-to-all-start = ((bf16[16,40,1280]{2,1,0:T(8,128)(2,1)}), bf16[16,40,1280]{2,1,0:T(8,128)(2,1)S(1)}, u32[]{:S(2)}, u32[]{:S(2)}) async-start(bf16[16,40,1280]{2,1,0:T(8,128)(2,1)} %broadcast_in_dim.74), calls=%async_computation | async-start | bytes 3276800 | tf_op jit(solution)/shard_map/all_to_all | solution.py:29
  19.8 47.4 %all-gather.20.cloned.1.call-done = bf16[2048,1280]{1,0:T(8,128)(2,1)} async-done(((bf16[128,1280]{1,0:T(8,128)(2,1)}), bf16[2048,1280]{1,0:T(8,128)(2,1)}) %all-gather.20.cloned.1.call-update) | async-done | bytes 5242896 | tf_op jit(solution)/shard_map/all_gather | solution.py:17
  67.2 5.3 fusion.48
  72.5 4.6 copy.72
  77.0 4.5 copy.71
  81.5 8.7 %fusion.49 = (f32[8,128]{1,0:T(8,128)S(1)}, f32[8,128,2048]{1,2,0:T(8,128)}) fusion(pred[128,2048]{0,1:T(8,128)(4,1)S(1)} %broadcast_compare_fusion, bf16[2048,8,80]{0,2,1:T(8,128)(2,1)} %bitcast.104, bf16[128,8,80]{0,2,1:T(8,128)(2,1)S(1)} %bitcast.118), kind=kOutput, calls=%fused_computation.96 | convolution fusion | flops 346032128 | bytes 11440128 | tf_op jit(solution)/shard_map/sub | solution.py:100
  90.2 5.2 fusion.30
  95.4 1.2 copy-done.1
  96.7 2.0 fusion.50
  99.1 0.9 reshape.203
  100.0 0.6 dynamic-slice
  101.4 8.4 %all-reduce = s32[512]{0:T(512)S(1)} all-reduce(s32[512]{0:T(512)S(1)} %bitcast_dynamic-update-slice_fusion), channel_id=2, replica_groups=mesh['section_0'=2,'section_1'=8,'fsdp_0'=2,'fsdp_1'=4,'fsdp_2'=2] {'fsd..., use_global_device_ids=true, to_apply=%add | all-reduce | flops 512 | bytes 4096 | tf_op jit(solution)/shard_map/all_gather | solution.py:148
  109.8 3.8 sort.31
  113.6 42.9 %all-gather.24.cloned.1.call-done = bf16[5120,256]{1,0:T(8,128)(2,1)} async-done(((bf16[320,256]{1,0:T(8,128)(2,1)}), bf16[5120,256]{1,0:T(8,128)(2,1)}) %all-gather.24.cloned.1.call-update) | async-done | bytes 2621456 | tf_op jit(solution)/shard_map/all_gather | solution.py:150
  156.5 44.9 %all-gather.22.cloned.1.call-done = bf16[512,5120]{1,0:T(8,128)(2,1)} async-done(((bf16[32,5120]{1,0:T(8,128)(2,1)}), bf16[512,5120]{1,0:T(8,128)(2,1)}) %all-gather.22.cloned.1.call-update) | async-done | bytes 5242896 | tf_op jit(solution)/shard_map/all_gather | solution.py:147
  201.4 4.8 convolution_convert_fusion.4
  206.2 2.6 gather_fusion.1
  208.8 3.8 all-to-all-start.1
  212.6 3.5 gather_fusion
  216.1 3.8 sort.32
  220.0 1.7 scatter_fusion
  222.0 1.8 fusion.26
  223.9 0.6 fusion.22
  224.5 0.7 gather_fusion.2
  225.2 0.7 copy.95
  225.9 5.7 %all-to-all-start.2 = ((bf16[32,16,256]{2,0,1:T(8,128)(2,1)}), bf16[32,16,256]{2,0,1:T(8,128)(2,1)S(1)}, u32[]{:S(2)}, u32[]{:S(2)}) async-start(bf16[32,16,256]{2,0,1:T(8,128)(2,1)} %bitcast.92), calls=%async_computation.2 | async-start | bytes 524288 | tf_op jit(solution)/shard_map/all_to_all | solution.py:173
  231.6 7.2 %all-to-all-done.2 = bf16[32,16,256]{2,0,1:T(8,128)(2,1)S(1)} async-done(((bf16[32,16,256]{2,0,1:T(8,128)(2,1)}), bf16[32,16,256]{2,0,1:T(8,128)(2,1)S(1)}, u32[]{:S(2)}, u32[]{:S(2)}) %all-to-all-start.2) | async-done | bytes 262176 | tf_op jit(solution)/shard_map/all_to_all | solution.py:173
  238.8 1.9 gather_fusion.3
  240.8 5.7 %convolution_convert_fusion = bf16[512,5120]{1,0:T(8,128)(2,1)} fusion(bf16[512,256]{1,0:T(8,128)(2,1)S(1)} %gather_fusion.3, bf16[5120,256]{1,0:T(8,128)(2,1)} %all-gather.24.cloned.1.call-done), kind=kOutput, calls=%fused_computation.13 | convolution fusion | flops 1344798720 | bytes 8126464 | tf_op jit(solution)/shard_map/dot_general | solution.py:176
  246.5 5.1 all-to-all-start.3
  251.6 4.1 convolution_convert_fusion.1
  255.7 1.7 copy.85
  257.6 63.6 %all-to-all-done.3 = bf16[16,32,5120]{2,1,0:T(8,128)(2,1)} async-done(((bf16[16,32,5120]{2,1,0:T(8,128)(2,1)}), bf16[16,32,5120]{2,1,0:T(8,128)(2,1)}, u32[]{:S(2)}, u32[]{:S(2)}) %all-to-all-start.3) | async-done | bytes 5242912 | tf_op jit(solution)/shard_map/all_to_all | solution.py:44
  321.2 3.5 convert_reduce_fusion
  325.5 2.2 convolution_convert_fusion.5
  327.9 6.5 %convolution_convert_fusion.3 = bf16[8,80,2048]{2,1,0:T(8,128)(2,1)} fusion(bf16[128,8,80]{0,2,1:T(8,128)(2,1)S(1)} %bitcast.114, f32[8,128,2048]{1,2,0:T(8,128)} %get-tuple-element.60, f32[8,128]{1,0:T(8,128)S(1)} %get-tuple-element.59), kind=kOutput, calls=%fused_computation.26 | convolution fusion | flops 341049344 | bytes 11177984 | tf_op jit(solution)/shard_map/hqk,qhd->khd/dot_general | solution.py:211
  334.4 3.1 copy.84
  337.5 6.4 %fusion.51 = f32[8,128,2048]{1,2,0:T(8,128)} fusion(bf16[128,8,80]{0,2,1:T(8,128)(2,1)S(1)} %bitcast.115, bf16[2048,8,80]{0,2,1:T(8,128)(2,1)} %bitcast.101), kind=kOutput, calls=%fused_computation.98 | convolution fusion | flops 335544320 | bytes 11173888 | tf_op jit(solution)/shard_map/qhd,khd->hqk/dot_general | solution.py:214
  344.0 14.6 %fusion.15 = bf16[8,2048,80]{1,2,0:T(8,128)(2,1)} fusion(bf16[128,8,80]{0,2,1:T(8,128)(2,1)S(1)} %bitcast.119, f32[8,128,2048]{1,2,0:T(8,128)} %fusion.51, f32[8,128,2048]{1,2,0:T(8,128)} %get-tuple-element.60, f32[8,128]{1,0:T(8,128)S(1)} %get-tuple-element.59), kind=kOutput, calls=%fused_computation.24 | convolution fusion | flops 351538176 | bytes 19566592 | tf_op jit(solution)/shard_map/hqk,qhd->khd/dot_general | solution.py:222
  358.6 4.4 copy.83
  363.0 4.4 pad_maximum_fusion
  368.1 28.9 %all_to_all.55 = bf16[16,40,1280]{2,1,0:T(8,128)(2,1)S(1)} all-to-all(bf16[16,40,1280]{2,1,0:T(8,128)(2,1)S(1)} %bitcast.102), channel_id=1, replica_groups=mesh['section_0'=2,'section_1'=8,'fsdp_0'=2,'fsdp_1'=4,'fsdp_2'=2] {'fsd..., dimensions={0} | all-to-all | bytes 3276800 | tf_op jit(solution)/shard_map/all_to_all | solution.py:44
  397.2 1.3 broadcast_in_dim.80
  398.5 9.2 %all-to-all-start.5 = ((bf16[16,40,1280]{2,1,0:T(8,128)(2,1)}), bf16[16,40,1280]{2,1,0:T(8,128)(2,1)S(1)}, u32[]{:S(2)}, u32[]{:S(2)}) async-start(bf16[16,40,1280]{2,1,0:T(8,128)(2,1)} %broadcast_in_dim.80), calls=%async_computation.8 | async-start | bytes 3276800 | tf_op jit(solution)/shard_map/all_to_all | solution.py:29
  407.7 5.7 %all-gather.1 = f32[8192]{0:T(1024)S(1)} all-gather(f32[4096]{0:T(1024)S(1)} %get-tuple-element.49), channel_id=3, replica_groups=mesh['section_0'=2,'section_1'=8,'fsdp_0'=2,'fsdp_1'=4,'fsdp_2'=2] {'sec..., dimensions={0}, use_global_device_ids=true | all-gather | bytes 49152 | tf_op jit(solution)/shard_map/all_gather | solution.py:68
  413.5 52.0 %all-gather.2 = f32[32768]{0:T(1024)S(1)} all-gather(f32[4096]{0:T(1024)S(1)} %reduce_sum.240), channel_id=4, replica_groups=mesh['section_0'=2,'section_1'=8,'fsdp_0'=2,'fsdp_1'=4,'fsdp_2'=2] {'sec..., dimensions={0}, use_global_device_ids=true | all-gather | bytes 147456 | tf_op jit(solution)/shard_map/all_gather | solution.py:68
  465.6 4.0 all-gather.3
  469.6 9.2 %all-gather.4 = f32[16384]{0:T(1024)S(1)} all-gather(f32[4096]{0:T(1024)S(1)} %reduce_sum.242), channel_id=6, replica_groups=mesh['section_0'=2,'section_1'=8,'fsdp_0'=2,'fsdp_1'=4,'fsdp_2'=2] {'fsd..., dimensions={0}, use_global_device_ids=true | all-gather | bytes 81920 | tf_op jit(solution)/shard_map/all_gather | solution.py:68
  478.9 8.2 %all-gather.5 = f32[8192]{0:T(1024)S(1)} all-gather(f32[4096]{0:T(1024)S(1)} %reduce_sum.243), channel_id=7, replica_groups=mesh['section_0'=2,'section_1'=8,'fsdp_0'=2,'fsdp_1'=4,'fsdp_2'=2] {'fsd..., dimensions={0}, use_global_device_ids=true | all-gather | bytes 49152 | tf_op jit(solution)/shard_map/all_gather | solution.py:68
  487.2 0.6 reduce_sum.244
  487.8 4.7 all-gather.11
  492.6 18.4 %all-gather.12 = f32[8,1,1280]{2,1,0:T(1,128)S(1)} all-gather(f32[1,1,1280]{2,1,0:T(1,128)S(1)} %reshape.273), channel_id=9, replica_groups=mesh['section_0'=2,'section_1'=8,'fsdp_0'=2,'fsdp_1'=4,'fsdp_2'=2] {'sec..., dimensions={0}, use_global_device_ids=true | all-gather | bytes 46080 | tf_op jit(solution)/shard_map/all_gather | solution.py:68
  511.0 3.2 all-gather.13
  514.3 9.1 %all-gather.14 = f32[4,1,1280]{2,1,0:T(1,128)S(1)} all-gather(f32[1,1,1280]{2,1,0:T(1,128)S(1)} %reshape.277), channel_id=11, replica_groups=mesh['section_0'=2,'section_1'=8,'fsdp_0'=2,'fsdp_1'=4,'fsdp_2'=2] {'fsd..., dimensions={0}, use_global_device_ids=true | all-gather | bytes 25600 | tf_op jit(solution)/shard_map/all_gather | solution.py:68
  523.4 13.6 %all-gather.15 = f32[2,1,1280]{2,1,0:T(1,128)S(1)} all-gather(f32[1,1,1280]{2,1,0:T(1,128)S(1)} %reshape.279), channel_id=12, replica_groups=mesh['section_0'=2,'section_1'=8,'fsdp_0'=2,'fsdp_1'=4,'fsdp_2'=2] {'fsd..., dimensions={0}, use_global_device_ids=true | all-gather | bytes 15360 | tf_op jit(solution)/shard_map/all_gather | solution.py:68
  537.1 0.6 reduce_sum.250
  537.7 14.3 %fusion.33 = bf16[8,80,128]{2,1,0:T(8,128)(2,1)S(1)} fusion(bf16[2048,8,80]{0,2,1:T(8,128)(2,1)} %bitcast.105, f32[8,128,2048]{1,2,0:T(8,128)} %fusion.51, f32[8,128,2048]{1,2,0:T(8,128)} %get-tuple-element.60, f32[8,128]{1,0:T(8,128)S(1)} %get-tuple-element.59), kind=kOutput, calls=%fused_computation.46 | convolution fusion | flops 350309376 | bytes 19566592 | tf_op jit(solution)/shard_map/hqk,khd->qhd/dot_general | solution.py:219
  552.0 0.8 copy.86
  552.8 1.7 bitcast_convert_fusion
  554.4 0.9 convert_reduce_fusion.1
  555.4 1.7 slice_bitcast_fusion
  (94 shorter events, 4.6 us)
Async XLA Ops:
  7.2 11.7 %copy-start.6 = (bf16[1,128,640]{2,1,0:T(8,128)(2,1)S(1)}, bf16[1,128,640]{2,1,0:T(8,128)(2,1)}, u32[]{:S(2)}) copy-start(bf16[1,128,640]{2,1,0:T(8,128)(2,1)} %param.13) | copy-start | bytes 491524
  7.2 11.9 %copy-start.11 = (s32[1,4]{1,0:T(1,128)S(1)}, s32[1,4]{1,0:T(1,128)}, u32[]{:S(2)}) copy-start(s32[1,4]{1,0:T(1,128)} %param.16) | copy-start | bytes 52
  7.2 60.0 %all-gather.20.cloned.1.call-start = ((), (), s32[]{:S(2)}) async-start(), calls=%async_computation.9 | async-start | bytes 5570560 | tf_op jit(solution)/shard_map/all_gather | solution.py:17
  9.0 147.4 %all-gather.24.cloned.1.call-start = ((), (), s32[]{:S(2)}) async-start(), calls=%async_computation.11 | async-start | bytes 2785280 | tf_op jit(solution)/shard_map/all_gather | solution.py:150
  12.0 83.5 %all-to-all-start = ((bf16[16,40,1280]{2,1,0:T(8,128)(2,1)}), bf16[16,40,1280]{2,1,0:T(8,128)(2,1)S(1)}, u32[]{:S(2)}, u32[]{:S(2)}) async-start(bf16[16,40,1280]{2,1,0:T(8,128)(2,1)} %broadcast_in_dim.74), calls=%async_computation | async-start | bytes 3276800 | tf_op jit(solution)/shard_map/all_to_all | solution.py:29
  18.8 182.6 %all-gather.22.cloned.1.call-start = ((), (), s32[]{:S(2)}) async-start(), calls=%async_computation.10 | async-start | bytes 5570560 | tf_op jit(solution)/shard_map/all_gather | solution.py:147
  19.0 62.5 %copy-start.7 = (bf16[1,128,640]{1,2,0:T(8,128)(2,1)}, bf16[1,128,640]{1,2,0:T(8,128)(2,1)S(1)}, u32[]{:S(2)}) copy-start(bf16[1,128,640]{1,2,0:T(8,128)(2,1)S(1)} %copy.73) | copy-start | bytes 491524
  90.2 6.5 %copy-start.5 = (bf16[1,128,1280]{2,1,0:T(8,128)(2,1)S(1)}, bf16[1,128,1280]{2,1,0:T(8,128)(2,1)}, u32[]{:S(2)}) copy-start(bf16[1,128,1280]{2,1,0:T(8,128)(2,1)} %param.12) | copy-start | bytes 983044
  90.2 8.7 %copy-start.9 = (f32[1280]{0:T(1024)S(1)}, f32[1280]{0:T(1024)}, u32[]{:S(2)}) copy-start(f32[1280]{0:T(1024)} %param.19) | copy-start | bytes 15364
  95.4 4.6 copy-start.13
  95.4 5.9 %copy-start.12 = (s32[1,32]{1,0:T(1,128)S(1)}, s32[1,32]{1,0:T(1,128)}, u32[]{:S(2)}) copy-start(s32[1,32]{1,0:T(1,128)} %param.17) | copy-start | bytes 388
  95.4 1.2 copy-start.1
  206.2 13.8 %copy-start = (bf16[1,128,4096]{2,1,0:T(8,128)(2,1)S(1)}, bf16[1,128,4096]{2,1,0:T(8,128)(2,1)}, u32[]{:S(2)}) copy-start(bf16[1,128,4096]{2,1,0:T(8,128)(2,1)} %param.21) | copy-start | bytes 3145732
  208.8 11.1 %all-to-all-start.1 = ((bf16[16,32,256]{2,1,0:T(8,128)(2,1)}), bf16[16,32,256]{2,1,0:T(8,128)(2,1)S(1)}, u32[]{:S(2)}, u32[]{:S(2)}) async-start(bf16[16,32,256]{2,1,0:T(8,128)(2,1)} %bitcast.15), calls=%async_computation.1 | async-start | bytes 524288 | tf_op jit(solution)/shard_map/all_to_all | solution.py:157
  212.5 9.5 %copy-start.2 = (bf16[1,128,4096]{2,1,0:T(8,128)(2,1)S(1)}, bf16[1,128,4096]{2,1,0:T(8,128)(2,1)}, u32[]{:S(2)}) copy-start(bf16[1,128,4096]{2,1,0:T(8,128)(2,1)} %param.23) | copy-start | bytes 3145732
  212.5 9.5 %copy-start.10 = (f32[4096]{0:T(1024)S(1)}, f32[4096]{0:T(1024)}, u32[]{:S(2)}) copy-start(f32[4096]{0:T(1024)} %param.22) | copy-start | bytes 49156
  221.7 2.2 copy-start.3
  225.9 12.9 %all-to-all-start.2 = ((bf16[32,16,256]{2,0,1:T(8,128)(2,1)}), bf16[32,16,256]{2,0,1:T(8,128)(2,1)S(1)}, u32[]{:S(2)}, u32[]{:S(2)}) async-start(bf16[32,16,256]{2,0,1:T(8,128)(2,1)} %bitcast.92), calls=%async_computation.2 | async-start | bytes 524288 | tf_op jit(solution)/shard_map/all_to_all | solution.py:173
  246.5 74.8 %all-to-all-start.3 = ((bf16[16,32,5120]{2,1,0:T(8,128)(2,1)}), bf16[16,32,5120]{2,1,0:T(8,128)(2,1)}, u32[]{:S(2)}, u32[]{:S(2)}) async-start(bf16[16,32,5120]{2,1,0:T(8,128)(2,1)} %bitcast.95), calls=%async_computation.3 | async-start | bytes 10485760 | tf_op jit(solution)/shard_map/all_to_all | solution.py:44
  251.5 111.4 %reduce-scatter.6.cloned.1.call-start = ((), (), s32[]{:S(2)}) async-start(), calls=%async_computation.13 | async-start | bytes 2949120 | tf_op jit(solution)/shard_map/reduce_scatter | solution.py:53
  257.3 295.4 %reduce-scatter.8.cloned.1.call-start = ((), (), s32[]{:S(2)}) async-start(), calls=%async_computation.14 | async-start | bytes 491520 | tf_op jit(solution)/shard_map/reduce_scatter | solution.py:53
  325.5 42.0 %copy-start.4 = (bf16[128,1280]{1,0:T(8,128)(2,1)}, bf16[128,1280]{1,0:T(8,128)(2,1)S(1)}, u32[]{:S(2)}) copy-start(bf16[128,1280]{1,0:T(8,128)(2,1)S(1)} %multiply_convert_fusion.1) | copy-start | bytes 983044
  337.5 6.4 %copy-start.8 = (bf16[1,128,640]{1,2,0:T(8,128)(2,1)S(1)}, bf16[1,128,640]{1,2,0:T(8,128)(2,1)}, u32[]{:S(2)}) copy-start(bf16[1,128,640]{1,2,0:T(8,128)(2,1)} %copy-done.7) | copy-start | bytes 491524
  363.0 192.4 %reduce-scatter.4.cloned.1.call-start = ((), (), s32[]{:S(2)}) async-start(), calls=%async_computation.12 | async-start | bytes 5570560 | tf_op jit(solution)/shard_map/reduce_scatter | solution.py:79
  398.5 155.9 %all-to-all-start.5 = ((bf16[16,40,1280]{2,1,0:T(8,128)(2,1)}), bf16[16,40,1280]{2,1,0:T(8,128)(2,1)S(1)}, u32[]{:S(2)}, u32[]{:S(2)}) async-start(bf16[16,40,1280]{2,1,0:T(8,128)(2,1)} %broadcast_in_dim.80), calls=%async_computation.8 | async-start | bytes 3276800 | tf_op jit(solution)/shard_map/all_to_all | solution.py:29
Sparse Core Ops, SparseCore 0:
  10.4 56.7 all-gather.19
  69.8 86.6 all-gather.23
  158.9 42.4 all-gather.21
  257.5 41.4 reduce-scatter.5
  363.1 36.0 reduce-scatter.7
  401.6 71.8 reduce-scatter.3
